TPU v7x, 32 devices: a whole 2x2x4 slice. The times are simulated.
32 devices in a mesh: side: 4 (over y, core), batch: 8 (over z, x).
Axes of the slice: x: 2, y: 2, z: 4, core: 2. Of those that a mesh axis runs over, the one named last changes fastest.
Arguments:
- hidden_in: bfloat16 [4, 8, 1024, 512], P('side', 'batch'), may hold values from -6 to 6
- segments: int32 [4, 8, 1024], P('side', 'batch'), may hold values from -1 to 31, as said below
- query_cls: int32 [8, 32], P('batch'), may hold values from 0 to 930, as said below
- passage_cls: int32 [4, 8, 5], P('side', 'batch'), may hold values from 0 to 800, as said below
- pair_passage: int32 [256], P('batch'), may hold values from 0 to 119
- passage_cluster: int32 [120], replicated, may hold values from 0 to 31
- teacher: float32 [256, 120], P('batch'), may hold values from -6 to 6
- query_weight: bfloat16 [512, 512], replicated, may hold values from -0.25 to 0.25
- query_bias: float32 [512], replicated, may hold values from -3 to 3
- key_weight: bfloat16 [512, 512], replicated, may hold values from -0.25 to 0.25
- value_weight: bfloat16 [512, 512], replicated, may hold values from -0.25 to 0.25
- value_bias: float32 [512], replicated, may hold values from -1.75 to 1.75
- out_weight: bfloat16 [512, 512], replicated, may hold values from -1 to 1
- out_bias: float32 [512], replicated, may hold values from -1.75 to 1.75
- first_gain: float32 [512], replicated, may hold values from 0.5 to 1.5
- first_shift: float32 [512], replicated, may hold values from -1.75 to 1.75
- inner_weight: bfloat16 [512, 2048], replicated, may hold values from -0.25 to 0.25
- inner_bias: float32 [2048], replicated, may hold values from -3 to 3
- outer_weight: bfloat16 [2048, 512], replicated, may hold values from -0.125 to 0.125
- outer_bias: float32 [512], replicated, may hold values from -1.75 to 1.75
- second_gain: float32 [512], replicated, may hold values from 0.5 to 1.5
- second_shift: float32 [512], replicated, may hold values from -1.75 to 1.75
Outputs:
- loss: float32 [], replicated
- rows_out: bfloat16 [4, 8, 1024, 512], P('side', 'batch')
- input_grad: bfloat16 [4, 8, 1024, 512], P('side', 'batch')
- grad_query_weight: float32 [512, 512], replicated
- grad_query_bias: float32 [512], replicated
- grad_key_weight: float32 [512, 512], replicated
- grad_value_weight: float32 [512, 512], replicated
- grad_value_bias: float32 [512], replicated
- grad_out_weight: float32 [512, 512], replicated
- grad_out_bias: float32 [512], replicated
- grad_first_gain: float32 [512], replicated
- grad_first_shift: float32 [512], replicated
- grad_inner_weight: float32 [512, 2048], replicated
- grad_inner_bias: float32 [2048], replicated
- grad_outer_weight: float32 [2048, 512], replicated
- grad_outer_bias: float32 [512], replicated
- grad_second_gain: float32 [512], replicated
- grad_second_shift: float32 [512], replicated
Inputs may be any that keep to these rules, and one draw needn't show every extreme that they name: `segments`: in every row segment numbers start at 0 and never fall; the tokens after the last segment carry -1. A row of the first group holds 32 queries of 8 to 30 tokens, one of exactly 30; a row of another group holds 5 passages of 50 to 200 tokens, one of exactly 200. `query_cls`: the first token of each segment of the first group's row, in order. `passage_cls`: the first token of each passage of the row, in order; in the first group it holds the first 5 query starts, which nothing uses.
All inputs are finite; a program needn't handle non-finite values.
Results may differ from a plain program's by a relative error of at most 0.02.
Values may be sent and summed in bfloat16 or wider, within the bound.
No kernel may reach another device: no remote copies, remote signals or barrier semaphores. Data moves between devices by JAX's collectives and lax.ppermute only.
A program may use at most 192 MiB of HBM per device.

v0:
```python
from functools import partial
import jax
import jax.numpy as jnp
from jax import lax
from jax.sharding import PartitionSpec as P

HEADS = 8
HD = 64
EPSILON = 1e-05
NEG_FILL = -1e30


def norm_forward(summed, gain, shift):
    centre = jnp.mean(summed, axis=1, keepdims=True)
    deviation = summed - centre
    inverse = lax.rsqrt(jnp.mean(deviation * deviation, axis=1, keepdims=True) + EPSILON)
    normed = deviation * inverse
    return (normed * gain + shift, normed, inverse)


def norm_backward(upstream, normed, inverse, gain):
    scaled_up = upstream * gain
    inner_mean = jnp.mean(scaled_up, axis=1, keepdims=True)
    cross_mean = jnp.mean(scaled_up * normed, axis=1, keepdims=True)
    grad_in = inverse * (scaled_up - inner_mean - normed * cross_mean)
    return (grad_in, jnp.sum(upstream * normed, axis=0), jnp.sum(upstream, axis=0))


def contract_rows(left, right):
    return lax.dot_general(
        left, right, (((0,), (0,)), ((), ())), preferred_element_type=jnp.float32
    )


def times_transposed(left, right):
    return lax.dot_general(
        left, right, (((1,), (1,)), ((), ())), preferred_element_type=jnp.float32
    )


def block_scores(query_part, keys3, seg_part, seg_all, score_scale):
    raw = (
        jnp.einsum("qhd,khd->hqk", query_part, keys3, preferred_element_type=jnp.float32)
        * score_scale
    )
    same = seg_part[:, None] == seg_all[None, :]
    return jnp.where(same[None], raw, NEG_FILL)


def body(
    hidden_in,
    segments,
    query_cls,
    passage_cls,
    pair_passage,
    passage_cluster,
    teacher,
    query_weight,
    query_bias,
    key_weight,
    value_weight,
    value_bias,
    out_weight,
    out_bias,
    first_gain,
    first_shift,
    inner_weight,
    inner_bias,
    outer_weight,
    outer_bias,
    second_gain,
    second_shift,
):
    count_tok = hidden_in.shape[2]
    model_width = hidden_in.shape[3]
    tokens = hidden_in.reshape(count_tok, model_width)
    seg_ids = segments.reshape(count_tok)
    query_idx = query_cls.reshape(-1)
    passage_idx = passage_cls.reshape(-1)
    is_query = lax.axis_index("side") == 0
    score_scale = HD ** (-0.5)
    cls_scale = model_width ** (-0.5)
    block_rows = min(512, count_tok)
    queries = (
        jnp.dot(tokens, query_weight, preferred_element_type=jnp.float32) + query_bias
    ).astype(jnp.bfloat16)
    keys_low = jnp.dot(tokens, key_weight, preferred_element_type=jnp.float32).astype(jnp.bfloat16)
    values_low = (
        jnp.dot(tokens, value_weight, preferred_element_type=jnp.float32) + value_bias
    ).astype(jnp.bfloat16)
    queries3 = queries.reshape(count_tok, HEADS, HD)
    keys3 = keys_low.reshape(count_tok, HEADS, HD)
    values3 = values_low.reshape(count_tok, HEADS, HD)
    contexts = []
    log_parts = []
    for first_row in range(0, count_tok, block_rows):
        scores = block_scores(
            queries3[first_row : first_row + block_rows],
            keys3,
            seg_ids[first_row : first_row + block_rows],
            seg_ids,
            score_scale,
        )
        peak = jnp.max(scores, axis=2, keepdims=True)
        expo = jnp.exp(scores - peak)
        total = jnp.sum(expo, axis=2, keepdims=True)
        probs_low = (expo / total).astype(jnp.bfloat16)
        contexts.append(
            jnp.einsum("hqk,khd->qhd", probs_low, values3, preferred_element_type=jnp.float32)
        )
        log_parts.append(peak + jnp.log(total))
    context_low = (
        jnp.concatenate(contexts, axis=0).reshape(count_tok, model_width).astype(jnp.bfloat16)
    )
    log_totals = jnp.concatenate(log_parts, axis=1)
    attended = tokens.astype(jnp.float32) + (
        jnp.dot(context_low, out_weight, preferred_element_type=jnp.float32) + out_bias
    )
    first, first_hat, first_inv = norm_forward(attended, first_gain, first_shift)
    first_low = first.astype(jnp.bfloat16)
    pre = jnp.dot(first_low, inner_weight, preferred_element_type=jnp.float32) + inner_bias
    gelu_exact = partial(jax.nn.gelu, approximate=False)
    activated, gelu_pull = jax.vjp(gelu_exact, pre)
    active_low = activated.astype(jnp.bfloat16)
    second = first + (
        jnp.dot(active_low, outer_weight, preferred_element_type=jnp.float32) + outer_bias
    )
    final, second_hat, second_inv = norm_forward(second, second_gain, second_shift)
    final_low = final.astype(jnp.bfloat16)
    query_vectors = final_low[query_idx]
    passage_vectors = final_low[passage_idx]
    gathered = lax.all_gather(passage_vectors, ("side", "batch"), axis=0, tiled=True)
    pass_count = teacher.shape[1]
    front = gathered.shape[0] - pass_count
    passages_all = gathered[front:]
    scores_cls = times_transposed(query_vectors, passages_all) * cls_scale
    columns = jnp.arange(pass_count, dtype=jnp.int32)
    is_pair = pair_passage[:, None] == columns[None, :]
    query_cluster = jnp.sum(jnp.where(is_pair, passage_cluster[None, :], 0), axis=1)
    counted = (
        (passage_cluster[None, :] == query_cluster[:, None]) & jnp.logical_not(is_pair) & is_query
    )
    pair_score = jnp.sum(jnp.where(is_pair, scores_cls, 0.0), axis=1, keepdims=True)
    resid = jnp.where(counted, pair_score - scores_cls - teacher, 0.0)
    loss_sq = jnp.sum(resid * resid)
    loss_count = jnp.sum(counted.astype(jnp.float32))
    grad_score = jnp.where(is_pair, jnp.sum(resid, axis=1, keepdims=True), 0.0) - resid
    grad_score_low = (grad_score * cls_scale).astype(jnp.bfloat16)
    grad_queries = jnp.dot(grad_score_low, passages_all, preferred_element_type=jnp.float32)
    padded = jnp.concatenate(
        [jnp.zeros((front, grad_score_low.shape[0]), jnp.bfloat16), grad_score_low.T], axis=0
    )
    grad_passages = lax.psum_scatter(
        jnp.dot(
            lax.slice_in_dim(
                padded, 0, passage_vectors.shape[0] * lax.axis_size(("side", "batch")), axis=0
            ),
            query_vectors,
            preferred_element_type=jnp.float32,
        ),
        ("side", "batch"),
        scatter_dimension=0,
        tiled=True,
    )
    zero_rows = jnp.zeros((count_tok, model_width), jnp.float32)
    grad_final = jnp.where(
        is_query,
        zero_rows.at[query_idx].add(grad_queries),
        zero_rows.at[passage_idx].add(grad_passages),
    )
    grad_second, grad_second_gain, grad_second_shift = norm_backward(
        grad_final, second_hat, second_inv, second_gain
    )
    grad_outer_bias = jnp.sum(grad_second, axis=0)
    second_low = grad_second.astype(jnp.bfloat16)
    grad_outer_weight = contract_rows(active_low, second_low)
    grad_active = times_transposed(second_low, outer_weight)
    grad_pre = gelu_pull(grad_active)[0]
    grad_inner_bias = jnp.sum(grad_pre, axis=0)
    pre_low = grad_pre.astype(jnp.bfloat16)
    grad_inner_weight = contract_rows(first_low, pre_low)
    grad_first = times_transposed(pre_low, inner_weight) + grad_second
    ffn_parts = (
        grad_inner_weight,
        grad_inner_bias,
        grad_outer_weight,
        grad_outer_bias,
        grad_second_gain,
        grad_second_shift,
    )
    grad_attended, grad_first_gain, grad_first_shift = norm_backward(
        grad_first, first_hat, first_inv, first_gain
    )
    grad_out_bias = jnp.sum(grad_attended, axis=0)
    attended_low = grad_attended.astype(jnp.bfloat16)
    grad_out_weight = contract_rows(context_low, attended_low)
    grad_context = times_transposed(attended_low, out_weight).astype(jnp.bfloat16)
    grad_context3 = grad_context.reshape(count_tok, HEADS, HD)
    grad_query_parts = []
    grad_keys = jnp.zeros((count_tok, HEADS, HD), jnp.float32)
    grad_values = jnp.zeros((count_tok, HEADS, HD), jnp.float32)
    for first_row in range(0, count_tok, block_rows):
        query_part = queries3[first_row : first_row + block_rows]
        scores = block_scores(
            query_part, keys3, seg_ids[first_row : first_row + block_rows], seg_ids, score_scale
        )
        probs = jnp.exp(scores - log_totals[:, first_row : first_row + block_rows])
        upstream = grad_context3[first_row : first_row + block_rows]
        grad_probs = jnp.einsum(
            "qhd,khd->hqk", upstream, values3, preferred_element_type=jnp.float32
        )
        row_dot = jnp.sum(probs * grad_probs, axis=2, keepdims=True)
        grad_scores = (probs * (grad_probs - row_dot)).astype(jnp.bfloat16)
        grad_query_parts.append(
            jnp.einsum("hqk,khd->qhd", grad_scores, keys3, preferred_element_type=jnp.float32)
            * score_scale
        )
        grad_keys = (
            grad_keys
            + jnp.einsum(
                "hqk,qhd->khd", grad_scores, query_part, preferred_element_type=jnp.float32
            )
            * score_scale
        )
        grad_values = grad_values + jnp.einsum(
            "hqk,qhd->khd", probs.astype(jnp.bfloat16), upstream, preferred_element_type=jnp.float32
        )
    grad_query = jnp.concatenate(grad_query_parts, axis=0).reshape(count_tok, model_width)
    grad_keys = grad_keys.reshape(count_tok, model_width)
    grad_values = grad_values.reshape(count_tok, model_width)
    grad_query_bias = jnp.sum(grad_query, axis=0)
    grad_value_bias = jnp.sum(grad_values, axis=0)
    query_low = grad_query.astype(jnp.bfloat16)
    key_low = grad_keys.astype(jnp.bfloat16)
    value_low = grad_values.astype(jnp.bfloat16)
    grad_query_weight = contract_rows(hidden_in.reshape(count_tok, model_width), query_low)
    grad_key_weight = contract_rows(tokens, key_low)
    grad_value_weight = contract_rows(tokens, value_low)
    input_grad = (
        grad_attended
        + times_transposed(query_low, query_weight)
        + times_transposed(key_low, key_weight)
        + times_transposed(value_low, value_weight)
    ).astype(jnp.bfloat16)
    attention_parts = (
        grad_query_weight,
        grad_query_bias,
        grad_key_weight,
        grad_value_weight,
        grad_value_bias,
        grad_out_weight,
        grad_out_bias,
        grad_first_gain,
        grad_first_shift,
    )
    summed_all = lax.psum(
        (
            grad_query_weight,
            grad_query_bias,
            grad_key_weight,
            grad_value_weight,
            grad_value_bias,
            grad_out_weight,
            grad_out_bias,
            grad_first_gain,
            grad_first_shift,
            grad_inner_weight,
            grad_inner_bias,
            grad_outer_weight,
            grad_outer_bias,
            grad_second_gain,
            grad_second_shift,
            loss_sq,
            loss_count,
        ),
        ("side", "batch"),
    )
    attention_parts = summed_all[:9]
    ffn_parts = summed_all[9:15]
    loss_sq = summed_all[15]
    loss_count = summed_all[16]
    loss = loss_sq / jnp.maximum(loss_count, 1.0)
    rows_out = final_low.reshape(1, 1, count_tok, model_width)
    input_grad = input_grad.reshape(1, 1, count_tok, model_width)
    return (
        loss,
        rows_out,
        input_grad,
        attention_parts[0],
        attention_parts[1],
        attention_parts[2],
        attention_parts[3],
        attention_parts[4],
        attention_parts[5],
        attention_parts[6],
        attention_parts[7],
        attention_parts[8],
        ffn_parts[0],
        ffn_parts[1],
        ffn_parts[2],
        ffn_parts[3],
        ffn_parts[4],
        ffn_parts[5],
    )


def solution(mesh):
    in_specs = (
        P("side", "batch", None, None),
        P("side", "batch", None),
        P("batch", None),
        P("side", "batch", None),
        P("batch"),
        P(),
        P("batch", None),
        P(),
        P(),
        P(),
        P(),
        P(),
        P(),
        P(),
        P(),
        P(),
        P(),
        P(),
        P(),
        P(),
        P(),
        P(),
    )
    out_specs = (
        P(),
        P("side", "batch", None, None),
        P("side", "batch", None, None),
        P(),
        P(),
        P(),
        P(),
        P(),
        P(),
        P(),
        P(),
        P(),
        P(),
        P(),
        P(),
        P(),
        P(),
        P(),
    )
    return jax.shard_map(body, mesh=mesh, in_specs=in_specs, out_specs=out_specs, check_vma=False)
```

profile of v0, /device:TPU:0, one launch (start us, length us, event | category | flops | bytes accessed | tf_op | source)
XLA Modules:
  0.0 664.5 jit_solution(5748049418920462220)
XLA Ops:
  16.4 3.2 fusion.79
  19.7 3.5 fusion.1
  25.4 3.8 fusion.35
  29.2 3.2 fusion.80
  32.4 3.5 fusion
  38.2 4.0 fusion.34
  44.5 23.8 %multiply_convert_fusion.2 = (bf16[1024,2048]{1,0:T(8,128)(2,1)S(1)}, f32[1024,2048]{1,0:T(8,128)}, f32[1024,2048]{1,0:T(8,128)}) fusion(f32[2048]{0:T(1024)S(1)} %copy-done.59, bf16[512,2048]{1,0:T(8,128)(2,1)S(1)} %copy-done, f32[1024,512]{0,1:T(8,128)S(1)} %get-tuple-element.126, f32[512]{0:T(512)S(1)} %copy-done.63, f32[512]{0:T(512)S(1)} %copy-done.53, ...), kind=kOutput, calls=%fused_computation.27 | convolution fusion | flops 2288517120 | bytes 25186304 | tf_op jit(solution)/shard_map/dot_general | solution.py:121
  68.4 2.7 fusion.82
  78.1 71.2 %all-gather.1 = bf16[32,5,512]{2,1,0:T(8,128)(2,1)S(1)} all-gather(bf16[1,5,512]{2,1,0:T(8,128)(2,1)S(1)} %bitcast.146), channel_id=2, replica_groups=mesh['side'=4,'batch'=8] {'side','batch'}, dimensions={0}, use_global_device_ids=true | all-gather | bytes 168960 | tf_op jit(solution)/shard_map/all_gather | solution.py:132
  155.1 2.9 copy.74
  158.1 115.9 %all-reduce.7.cloned.1.call-done = f32[160,512]{1,0:T(8,128)} async-done(((f32[160,512]{1,0:T(8,128)}), f32[160,512]{1,0:T(8,128)}) %all-reduce.7.cloned.1.call-update) | async-done | bytes 327696
  276.2 3.0 copy.75
  279.3 3.9 multiply_reduce_fusion.2
  285.4 4.5 fusion.52
  289.9 9.7 %fusion.83 = (f32[2048]{0:T(1024)}, bf16[1024,2048]{1,0:T(8,128)(2,1)S(1)}) fusion(f32[1024,2048]{1,0:T(8,128)} %get-tuple-element.108, bf16[2048,512]{1,0:T(8,128)(2,1)S(1)} %copy-done.58, f32[1024,512]{0,1:T(8,128)S(1)} %get-tuple-element.102, f32[1024,2048]{1,0:T(8,128)} %get-tuple-element.127, f32[2048]{0:T(1024)S(1)} %copy-done.59), kind=kOutput, calls=%fused_computation.157 | convolution fusion | flops 2181560320 | bytes 25182208 | tf_op jit(solution)/shard_map/dot_general | solution.py:36
  299.6 3.7 multiply_reduce_fusion.3
  303.3 4.5 fusion.18
  313.1 9.9 %multiply_reduce_fusion.1 = (f32[8,512]{1,0:T(8,128)}, f32[8,512,1024]{2,1,0:T(8,128)}) fusion(f32[8,512,1024]{2,1,0:T(8,128)S(1)} %bitcast.120, f32[8,512]{1,0:T(8,128)S(1)} %log_add_fusion.1, bf16[512,8,64]{0,2,1:T(8,128)(2,1)S(1)} %bitcast.131, bf16[1024,8,64]{0,2,1:T(8,128)(2,1)} %bitcast.137), kind=kOutput, calls=%fused_computation.8 | convolution fusion | flops 549449728 | bytes 35160064 | tf_op jit(solution)/shard_map/qhd,khd->hqk/dot_general | solution.py:209
  323.0 15.9 %multiply_convert_fusion.1 = bf16[8,512,1024]{2,1,0:T(8,128)(2,1)} fusion(f32[8,512,1024]{2,1,0:T(8,128)} %get-tuple-element.133, f32[8,512,1024]{2,1,0:T(8,128)} %copy-done.2, f32[8,512]{1,0:T(8,128)} %get-tuple-element.132, f32[8,512]{1,0:T(8,128)S(1)} %log_add_fusion.1), kind=kLoop, calls=%fused_computation.7 | loop fusion | flops 16777216 | bytes 41975808 | tf_op jit(solution)/shard_map/convert_element_type | solution.py:213
  338.9 8.2 %fusion.74 = (bf16[512,8,64]{0,2,1:T(8,128)(2,1)}, f32[8,64]{1,0:T(8,128)}) fusion(bf16[1024,8,64]{0,2,1:T(8,128)(2,1)S(1)} %bitcast.124, bf16[8,512,1024]{2,1,0:T(8,128)(2,1)} %multiply_convert_fusion.1), kind=kOutput, calls=%fused_computation.148 | convolution fusion | flops 537656832 | bytes 9963520 | tf_op jit(solution)/shard_map/hqk,khd->qhd/dot_general | solution.py:215
  347.2 6.3 fusion.84
  353.6 4.0 fusion.5
  357.6 9.9 %multiply_reduce_fusion = (f32[8,512]{1,0:T(8,128)}, f32[8,512,1024]{2,1,0:T(8,128)}) fusion(f32[8,512,1024]{2,1,0:T(8,128)S(1)} %bitcast.118, f32[8,512]{1,0:T(8,128)} %log_add_fusion, bf16[512,8,64]{0,2,1:T(8,128)(2,1)} %bitcast.133, bf16[1024,8,64]{0,2,1:T(8,128)(2,1)} %bitcast.138), kind=kOutput, calls=%fused_computation.5 | convolution fusion | flops 549449728 | bytes 35160064 | tf_op jit(solution)/shard_map/qhd,khd->hqk/dot_general | solution.py:209
  367.5 8.8 %bitcast_reduce_fusion = (f32[8,64]{1,0:T(8,128)}, bf16[8,64,1024]{2,1,0:T(8,128)(2,1)S(1)}) fusion(f32[8,64,1024]{2,1,0:T(8,128)} %fusion.5, bf16[512,8,64]{0,2,1:T(8,128)(2,1)S(1)} %bitcast.132, f32[8,512,1024]{2,1,0:T(8,128)} %copy-done.2, f32[8,512]{1,0:T(8,128)S(1)} %log_add_fusion.1), kind=kOutput, calls=%fused_computation.43 | convolution fusion | flops 546831872 | bytes 20465664 | tf_op jit(solution)/shard_map/hqk,qhd->khd/dot_general | solution.py:225
  378.1 10.5 %multiply_convert_fusion = bf16[8,512,1024]{2,1,0:T(8,128)(2,1)} fusion(f32[8,512,1024]{2,1,0:T(8,128)} %get-tuple-element.135, f32[8,512,1024]{2,1,0:T(8,128)S(1)} %bitcast.118, f32[8,512]{1,0:T(8,128)S(1)} %copy-done.38, f32[8,512]{1,0:T(8,128)S(1)} %copy-done.37), kind=kLoop, calls=%fused_computation.4 | loop fusion | flops 16777216 | bytes 41975808 | tf_op jit(solution)/shard_map/convert_element_type | solution.py:213
  388.6 6.6 fusion.75
  395.3 3.4 multiply_convert_fusion.3
  402.8 2.9 fusion.134
  408.2 43.7 %all-reduce.2 = (f32[]{:T(128)}, f32[]{:T(128)}, f32[512]{0:T(512)}, f32[512]{0:T(512)}, f32[512]{0:T(512)}, /*index=5*/f32[512]{0:T(512)}, f32[512]{0:T(512)}, ...) all-reduce(f32[]{:T(128)} %get-tuple-element.81, ...), channel_id=1, replica_groups=mesh['side'=4,'batch'=8] {'side','batch'}, use_global_device_ids=true, to_apply=%region_11.12 | all-reduce | flops 6146 | bytes 49168 | tf_op jit(solution)/shard_map/psum | solution.py:256
  459.4 181.1 %all-reduce.9.cloned.1.call-done = (f32[512,512]{0,1:T(8,128)}, f32[512,512]{0,1:T(8,128)}, f32[512,512]{0,1:T(8,128)}, f32[512,512]{1,0:T(8,128)}, f32[512,2048]{1,0:T(8,128)}, /*index=5*/f32[2048,512]{1,0:T(8,128)}) async-done(((f32[512,512]{0,1:T(8,128)}, f32[512,512]{0,1:T(8,128)}, f32[512,512]{0,1:T(8,128)}, f32[512,512]{1,0:T(8,128)}, f32[512,2048]{1,0:T(8,128)}, /*index=5*/f32[2048,512]{1,0:T(8,128)}), ...) | async-done | bytes 12582928 | tf_op jit(solution)/shard_map/psum | solution.py:256
  640.5 2.6 copy.82
  649.2 4.8 copy.98
  (213 shorter events, 60.6 us)
Async XLA Ops:
  7.2 37.3 %copy-start = (bf16[512,2048]{1,0:T(8,128)(2,1)S(1)}, bf16[512,2048]{1,0:T(8,128)(2,1)}, u32[]{:S(2)}) copy-start(bf16[512,2048]{1,0:T(8,128)(2,1)} %param.38) | copy-start | bytes 6291460
  7.2 6.9 %copy-start.25 = (bf16[1,1,1024,512]{3,2,1,0:T(8,128)(2,1)S(1)}, bf16[1,1,1024,512]{3,2,1,0:T(8,128)(2,1)}, u32[]{:S(2)}) copy-start(bf16[1,1,1024,512]{3,2,1,0:T(8,128)(2,1)} %param.22) | copy-start | bytes 3145732
  7.2 266.8 %all-reduce.7.cloned.1.call-start = ((), (), s32[]{:S(2)}) async-start(), calls=%async_computation | async-start | bytes 655360
  14.2 15.0 %copy-start.14 = (bf16[512,512]{0,1:T(8,128)(2,1)}, bf16[512,512]{0,1:T(8,128)(2,1)S(1)}, u32[]{:S(2)}) copy-start(bf16[512,512]{0,1:T(8,128)(2,1)S(1)} %get-tuple-element.115) | copy-start | bytes 1572868
  15.0 14.3 %copy-start.8 = (bf16[1024,512]{0,1:T(8,128)(2,1)}, bf16[1024,512]{0,1:T(8,128)(2,1)S(1)}, u32[]{:S(2)}) copy-start(bf16[1024,512]{0,1:T(8,128)(2,1)S(1)} %convolution_convert_fusion.1) | copy-start | bytes 3145732
  15.7 20.2 %copy-start.17 = (bf16[1024,512]{0,1:T(8,128)(2,1)}, bf16[1024,512]{0,1:T(8,128)(2,1)S(1)}, u32[]{:S(2)}) copy-start(bf16[1024,512]{0,1:T(8,128)(2,1)S(1)} %add_convert_fusion.3) | copy-start | bytes 3145732
  19.7 5.7 copy-start.1
  32.4 5.7 copy-start.2
  44.1 24.2 %copy-start.10 = (f32[1024,512]{0,1:T(8,128)}, f32[1024,512]{0,1:T(8,128)S(1)}, u32[]{:S(2)}) copy-start(f32[1024,512]{0,1:T(8,128)S(1)} %get-tuple-element.126) | copy-start | bytes 6291460
  44.5 23.9 %copy-start.57 = (bf16[2048,512]{1,0:T(8,128)(2,1)S(1)}, bf16[2048,512]{1,0:T(8,128)(2,1)}, u32[]{:S(2)}) copy-start(bf16[2048,512]{1,0:T(8,128)(2,1)} %param.40) | copy-start | bytes 6291460
  44.5 23.9 %copy-start.62 = (f32[512]{0:T(512)S(1)}, f32[512]{0:T(512)}, u32[]{:S(2)}) copy-start(f32[512]{0:T(512)} %param.41) | copy-start | bytes 6148
  71.1 78.2 %copy-start.52 = (s32[32]{0:T(128)S(1)}, s32[32]{0:T(128)}, u32[]{:S(2)}) copy-start(s32[32]{0:T(128)} %param.26) | copy-start | bytes 388
  71.2 78.2 %copy-start.56 = (s32[120]{0:T(128)S(1)}, s32[120]{0:T(128)}, u32[]{:S(2)}) copy-start(s32[120]{0:T(128)} %param.27) | copy-start | bytes 1444
  71.2 79.1 %copy-start.44 = (f32[32,120]{1,0:T(8,128)S(1)}, f32[32,120]{1,0:T(8,128)}, u32[]{:S(2)}) copy-start(f32[32,120]{1,0:T(8,128)} %param.28) | copy-start | bytes 46084
  152.1 488.4 %all-reduce.9.cloned.1.call-start = ((), (), s32[]{:S(2)}) async-start(), calls=%async_computation.1 | async-start | bytes 25165824 | tf_op jit(solution)/shard_map/psum | solution.py:256
  289.9 9.7 %copy-start.11 = (f32[1024,512]{0,1:T(8,128)S(1)}, f32[1024,512]{0,1:T(8,128)}, u32[]{:S(2)}) copy-start(f32[1024,512]{0,1:T(8,128)} %copy-done.10) | copy-start | bytes 6291460
  303.3 9.3 %slice-start.4 = ((s8[16777216]{0:T(1024)(128)(4,1)}), s8[4194304]{0:T(1024)(128)(4,1)S(1)}, s32[]{:S(2)}) async-start(s8[16777216]{0:T(1024)(128)(4,1)} %bitcast.119), calls=%async_computation.6 | async-start | bytes 8388608
  303.3 9.3 %slice-start.5 = ((s8[16777216]{0:T(1024)(128)(4,1)}), s8[4194304]{0:T(1024)(128)(4,1)S(1)}, s32[]{:S(2)}) async-start(s8[16777216]{0:T(1024)(128)(4,1)} %bitcast.119), calls=%async_computation.7 | async-start | bytes 8388608
  322.9 16.0 %copy-start.9 = (bf16[1024,512]{0,1:T(8,128)(2,1)S(1)}, bf16[1024,512]{0,1:T(8,128)(2,1)}, u32[]{:S(2)}) copy-start(bf16[1024,512]{0,1:T(8,128)(2,1)} %copy-done.8) | copy-start | bytes 3145732
  322.9 30.6 %slice-start = ((s8[16777216]{0:T(1024)(128)(4,1)}), s8[4194304]{0:T(1024)(128)(4,1)S(1)}, s32[]{:S(2)}) async-start(s8[16777216]{0:T(1024)(128)(4,1)} %bitcast.117), calls=%async_computation.2 | async-start | bytes 8388608
  322.9 30.6 %slice-start.1 = ((s8[16777216]{0:T(1024)(128)(4,1)}), s8[4194304]{0:T(1024)(128)(4,1)S(1)}, s32[]{:S(2)}) async-start(s8[16777216]{0:T(1024)(128)(4,1)} %bitcast.117), calls=%async_computation.3 | async-start | bytes 8388608
  323.0 30.6 %slice-start.2 = ((s8[16777216]{0:T(1024)(128)(4,1)}), s8[4194304]{0:T(1024)(128)(4,1)S(1)}, s32[]{:S(2)}) async-start(s8[16777216]{0:T(1024)(128)(4,1)} %bitcast.117), calls=%async_computation.4 | async-start | bytes 8388608
  338.9 8.2 %copy-start.15 = (bf16[512,512]{0,1:T(8,128)(2,1)S(1)}, bf16[512,512]{0,1:T(8,128)(2,1)}, u32[]{:S(2)}) copy-start(bf16[512,512]{0,1:T(8,128)(2,1)} %copy-done.14) | copy-start | bytes 1572868
  338.9 14.6 %slice-start.3 = ((s8[16777216]{0:T(1024)(128)(4,1)}), s8[4194304]{0:T(1024)(128)(4,1)S(1)}, s32[]{:S(2)}) async-start(s8[16777216]{0:T(1024)(128)(4,1)} %bitcast.117), calls=%async_computation.5 | async-start | bytes 8388608
  347.2 6.4 copy-start.16
  347.2 6.4 copy-start.36
  367.5 8.8 %copy-start.26 = (bf16[1,1,1024,512]{3,2,1,0:T(8,128)(2,1)S(1)}, bf16[1,1,1024,512]{3,2,1,0:T(8,128)(2,1)}, u32[]{:S(2)}) copy-start(bf16[1,1,1024,512]{3,2,1,0:T(8,128)(2,1)} %param.22) | copy-start | bytes 3145732
  367.5 10.6 %copy-start.37 = (f32[8,512]{1,0:T(8,128)S(1)}, f32[8,512]{1,0:T(8,128)}, u32[]{:S(2)}) copy-start(f32[8,512]{1,0:T(8,128)} %log_add_fusion) | copy-start | bytes 49156
  367.5 10.6 %copy-start.38 = (f32[8,512]{1,0:T(8,128)S(1)}, f32[8,512]{1,0:T(8,128)}, u32[]{:S(2)}) copy-start(f32[8,512]{1,0:T(8,128)} %get-tuple-element.134) | copy-start | bytes 49156
  388.6 6.6 copy-start.3
  388.6 6.6 copy-start.13
  640.5 7.7 %copy-start.28 = (f32[512,512]{1,0:T(8,128)S(1)}, f32[512,512]{1,0:T(8,128)}, u32[]{:S(2)}) copy-start(f32[512,512]{1,0:T(8,128)} %get-tuple-element.156) | copy-start | bytes 3145732
  (44 other events, 160.4 us)
Sparse Core Ops, SparseCore 0:
  152.2 121.7 all-reduce.6
  402.2 238.2 all-reduce.8
where the time goes:
time: 674 us; the launch traced here: 664 us
  waiting for transfers between devices  297 us (44%)
  matrix products  138 us (20%)
  blocking collectives  115 us (17%)
  other arithmetic  53.7 us (8%)
  local copies, waits for them, and re-layouts  43.2 us (6%)
  between operations  17.9 us (3%)
    psum x1, waiting for transfers between devices, body(): lax.psum((grad_query_weight, grad_query_bias, grad_key_weight, grad_value...  181 us
    unnamed x3, waiting for transfers between devices  116 us
    all_gather x1, blocking collectives, body(): lax.all_gather(passage_vectors, ('side', 'batch'), axis=0, tiled=True)  71.2 us
    psum x1, blocking collectives, body(): lax.psum((grad_query_weight, grad_query_bias, grad_key_weight, grad_value...  43.7 us
    unnamed x157, local copies, waits for them, and re-layouts  30.1 us
    convert_element_type x2, other arithmetic, body(): grad_scores = (probs * (grad_probs - row_dot)).astype(jnp.bfloat16)  26.4 us
    dot_general x1, matrix products, body(): jnp.dot(first_low, inner_weight, preferred_element_type=jnp.float32)  23.8 us
    dot_general x2, matrix products, body(): jnp.einsum('qhd,khd->hqk', upstream, values3, preferred_element_type=jnp....  19.8 us
  transfers between devices with their start and end apart: 2, of which 2 were waited for; matrix products, arithmetic and copies ran while one was open for 3% of the time, Pallas kernels for 0%

commit v1 on v0

--- a/solution.py
+++ b/solution.py
@@ -254,26 +254,29 @@
         grad_first_shift,
     )
     summed_all = lax.psum(
-        (
-            grad_query_weight,
-            grad_query_bias,
-            grad_key_weight,
-            grad_value_weight,
-            grad_value_bias,
-            grad_out_weight,
-            grad_out_bias,
-            grad_first_gain,
-            grad_first_shift,
-            grad_inner_weight,
-            grad_inner_bias,
-            grad_outer_weight,
-            grad_outer_bias,
-            grad_second_gain,
-            grad_second_shift,
-            loss_sq,
-            loss_count,
+        lax.psum(
+            (
+                grad_query_weight,
+                grad_query_bias,
+                grad_key_weight,
+                grad_value_weight,
+                grad_value_bias,
+                grad_out_weight,
+                grad_out_bias,
+                grad_first_gain,
+                grad_first_shift,
+                grad_inner_weight,
+                grad_inner_bias,
+                grad_outer_weight,
+                grad_outer_bias,
+                grad_second_gain,
+                grad_second_shift,
+                loss_sq,
+                loss_count,
+            ),
+            "batch",
         ),
-        ("side", "batch"),
+        "side",
     )
     attention_parts = summed_all[:9]
     ffn_parts = summed_all[9:15]

time: 674 us -> 1060 us (1.57)
  waiting for transfers between devices: 297 us -> 683 us
    psum x1, waiting for transfers between devices: 181 us -> 404 us  [body(): lax.psum((grad_query_weight, grad_query_bias, grad_key_weight, grad_value...]
    psum x0 -> x1, waiting for transfers between devices: none -> 163 us  [body(): lax.psum(lax.psum((grad_query_weight, grad_query_bias, grad_key_weight, g...]
    psum x0 -> x1, blocking collectives: none -> 13 us  [body(): lax.psum(lax.psum((grad_query_weight, grad_query_bias, grad_key_weight, g...]
    unnamed x157 -> x163, local copies, waits for them, and re-layouts: 30.1 us -> 29.9 us
    unnamed x3 -> x4, waiting for transfers between devices: 116 us -> 116 us
  transfers between devices with their start and end apart: 2 -> 3, of which waited for: 2 -> 3; matrix products, arithmetic and copies ran while one was open for 3% -> 2% of each run, Pallas kernels for 0% -> 0%
where the time goes in v1:
time: 1060 us; the launch traced here: 1050 us
  waiting for transfers between devices  683 us (64%)
  matrix products  138 us (13%)
  blocking collectives  119 us (11%)
  other arithmetic  52.1 us (5%)
  local copies, waits for them, and re-layouts  42.9 us (4%)
  between operations  17.6 us (2%)
    psum x1, waiting for transfers between devices, body(): lax.psum((grad_query_weight, grad_query_bias, grad_key_weight, grad_value...  404 us
    psum x1, waiting for transfers between devices, body(): lax.psum(lax.psum((grad_query_weight, grad_query_bias, grad_key_weight, g...  163 us
    unnamed x4, waiting for transfers between devices  116 us
    all_gather x1, blocking collectives, body(): lax.all_gather(passage_vectors, ('side', 'batch'), axis=0, tiled=True)  71.2 us
    psum x1, blocking collectives, body(): lax.psum((grad_query_weight, grad_query_bias, grad_key_weight, grad_value...  34.5 us
    unnamed x163, local copies, waits for them, and re-layouts  29.9 us
    convert_element_type x2, other arithmetic, body(): grad_scores = (probs * (grad_probs - row_dot)).astype(jnp.bfloat16)  26.4 us
    dot_general x1, matrix products, body(): jnp.dot(first_low, inner_weight, preferred_element_type=jnp.float32)  23.8 us
  transfers between devices with their start and end apart: 3, of which 3 were waited for; matrix products, arithmetic and copies ran while one was open for 2% of the time, Pallas kernels for 0%

profile of v1, /device:TPU:0, one launch (start us, length us, event | category | flops | bytes accessed | tf_op | source)
XLA Modules:
  0.0 1052.4 jit_solution(1884869944631554155)
XLA Ops:
  16.4 3.2 fusion.79
  19.7 3.5 fusion.1
  25.4 3.8 fusion.35
  29.2 3.2 fusion.80
  32.4 3.5 fusion
  38.2 4.0 fusion.34
  44.5 23.8 %multiply_convert_fusion.2 = (bf16[1024,2048]{1,0:T(8,128)(2,1)S(1)}, f32[1024,2048]{1,0:T(8,128)}, f32[1024,2048]{1,0:T(8,128)}) fusion(f32[2048]{0:T(1024)S(1)} %copy-done.62, bf16[512,2048]{1,0:T(8,128)(2,1)S(1)} %copy-done, f32[1024,512]{0,1:T(8,128)S(1)} %get-tuple-element.143, f32[512]{0:T(512)S(1)} %copy-done.66, f32[512]{0:T(512)S(1)} %copy-done.56, ...), kind=kOutput, calls=%fused_computation.27 | convolution fusion | flops 2288517120 | bytes 25186304 | tf_op jit(solution)/shard_map/dot_general | solution.py:121
  78.1 71.2 %all-gather.1 = bf16[32,5,512]{2,1,0:T(8,128)(2,1)S(1)} all-gather(bf16[1,5,512]{2,1,0:T(8,128)(2,1)S(1)} %bitcast.146), channel_id=2, replica_groups=mesh['side'=4,'batch'=8] {'side','batch'}, dimensions={0}, use_global_device_ids=true | all-gather | bytes 168960 | tf_op jit(solution)/shard_map/all_gather | solution.py:132
  155.2 2.9 copy.74
  158.1 115.9 %all-reduce.10.cloned.1.call-done = f32[160,512]{1,0:T(8,128)} async-done(((f32[160,512]{1,0:T(8,128)}), f32[160,512]{1,0:T(8,128)}) %all-reduce.10.cloned.1.call-update) | async-done | bytes 327696
  276.2 3.0 copy.75
  279.3 3.9 multiply_reduce_fusion.2
  285.3 4.5 fusion.52
  289.9 9.7 fusion.83
  299.6 3.7 multiply_reduce_fusion.3
  303.3 4.5 fusion.18
  313.1 9.3 multiply_reduce_fusion.1
  322.4 15.9 %multiply_convert_fusion.1 = bf16[8,512,1024]{2,1,0:T(8,128)(2,1)} fusion(f32[8,512,1024]{2,1,0:T(8,128)} %get-tuple-element.150, f32[8,512,1024]{2,1,0:T(8,128)} %copy-done.3, f32[8,512]{1,0:T(8,128)S(1)} %get-tuple-element.149, f32[8,512]{1,0:T(8,128)S(1)} %log_add_fusion.1), kind=kLoop, calls=%fused_computation.7 | loop fusion | flops 16777216 | bytes 41975808 | tf_op jit(solution)/shard_map/convert_element_type | solution.py:213
  338.3 8.2 fusion.74
  346.5 6.3 fusion.84
  352.9 4.0 fusion.5
  356.9 9.8 multiply_reduce_fusion
  366.8 8.8 bitcast_reduce_fusion
  377.3 10.5 multiply_convert_fusion
  387.8 6.3 fusion.75
  394.2 3.4 multiply_convert_fusion.3
  401.0 403.9 %all-reduce.12.cloned.1.call-done = (f32[512,512]{0,1:T(8,128)}, f32[512,512]{0,1:T(8,128)}, f32[512,512]{0,1:T(8,128)}, f32[512,512]{1,0:T(8,128)}, f32[512,2048]{1,0:T(8,128)}, /*index=5*/f32[2048,512]{1,0:T(8,128)}) async-done(((f32[512,512]{0,1:T(8,128)}, f32[512,512]{0,1:T(8,128)}, f32[512,512]{0,1:T(8,128)}, f32[512,512]{1,0:T(8,128)}, f32[512,2048]{1,0:T(8,128)}, /*index=5*/f32[2048,512]{1,0:T(8,128)}), ...) | async-done | bytes 12582928 | tf_op jit(solution)/shard_map/psum | solution.py:257
  810.4 34.5 %all-reduce.2 = (f32[]{:T(128)}, f32[]{:T(128)}, f32[512]{0:T(512)S(1)}, f32[512]{0:T(512)S(1)}, f32[512]{0:T(512)S(1)}, /*index=5*/f32[512]{0:T(512)S(1)}, f32[...) all-reduce(f32[]{:T(128)} %get-tuple-element.81, ...), channel_id=1, replica_groups=mesh['side'=4,'batch'=8] {'batch'}, use_global_device_ids=true, to_apply=%region_11.12 | all-reduce | flops 6146 | bytes 49168 | tf_op jit(solution)/shard_map/psum | solution.py:257
  844.9 13.0 %all-reduce.4 = (f32[]{:T(128)}, f32[]{:T(128)}, f32[512]{0:T(512)}, f32[512]{0:T(512)}, f32[512]{0:T(512)}, /*index=5*/f32[512]{0:T(512)}, f32[512]{0:T(512)}, ...) all-reduce(f32[]{:T(128)} %get-tuple-element.84, ...), channel_id=1, replica_groups=mesh['side'=4,'batch'=8] {'side'}, use_global_device_ids=true, to_apply=%region_12.13 | all-reduce | flops 6146 | bytes 49168 | tf_op jit(solution)/shard_map/psum | solution.py:256
  866.5 163.4 %all-reduce.14.cloned.1.call-done = (f32[512,512]{0,1:T(8,128)}, f32[512,512]{0,1:T(8,128)}, f32[512,512]{0,1:T(8,128)}, f32[512,512]{1,0:T(8,128)}, f32[512,2048]{1,0:T(8,128)}, /*index=5*/f32[2048,512]{1,0:T(8,128)}) async-done(((f32[512,512]{0,1:T(8,128)}, f32[512,512]{0,1:T(8,128)}, f32[512,512]{0,1:T(8,128)}, f32[512,512]{1,0:T(8,128)}, f32[512,2048]{1,0:T(8,128)}, /*index=5*/f32[2048,512]{1,0:T(8,128)}), ...) | async-done | bytes 12582928 | tf_op jit(solution)/shard_map/psum | solution.py:256
  1029.9 2.7 copy.82
  1037.4 4.8 copy.104
  (223 shorter events, 65.5 us)
Async XLA Ops:
  7.2 37.3 %copy-start = (bf16[512,2048]{1,0:T(8,128)(2,1)S(1)}, bf16[512,2048]{1,0:T(8,128)(2,1)}, u32[]{:S(2)}) copy-start(bf16[512,2048]{1,0:T(8,128)(2,1)} %param.38) | copy-start | bytes 6291460
  7.2 6.9 copy-start.27
  7.2 266.8 %all-reduce.10.cloned.1.call-start = ((), (), s32[]{:S(2)}) async-start(), calls=%async_computation | async-start | bytes 655360
  14.2 15.0 %copy-start.16 = (bf16[512,512]{0,1:T(8,128)(2,1)}, bf16[512,512]{0,1:T(8,128)(2,1)S(1)}, u32[]{:S(2)}) copy-start(bf16[512,512]{0,1:T(8,128)(2,1)S(1)} %get-tuple-element.132) | copy-start | bytes 1572868
  15.0 14.3 %copy-start.10 = (bf16[1024,512]{0,1:T(8,128)(2,1)}, bf16[1024,512]{0,1:T(8,128)(2,1)S(1)}, u32[]{:S(2)}) copy-start(bf16[1024,512]{0,1:T(8,128)(2,1)S(1)} %convolution_convert_fusion.1) | copy-start | bytes 3145732
  15.7 20.2 %copy-start.19 = (bf16[1024,512]{0,1:T(8,128)(2,1)}, bf16[1024,512]{0,1:T(8,128)(2,1)S(1)}, u32[]{:S(2)}) copy-start(bf16[1024,512]{0,1:T(8,128)(2,1)S(1)} %add_convert_fusion.3) | copy-start | bytes 3145732
  44.2 24.2 %copy-start.12 = (f32[1024,512]{0,1:T(8,128)}, f32[1024,512]{0,1:T(8,128)S(1)}, u32[]{:S(2)}) copy-start(f32[1024,512]{0,1:T(8,128)S(1)} %get-tuple-element.143) | copy-start | bytes 6291460
  44.5 23.9 %copy-start.60 = (bf16[2048,512]{1,0:T(8,128)(2,1)S(1)}, bf16[2048,512]{1,0:T(8,128)(2,1)}, u32[]{:S(2)}) copy-start(bf16[2048,512]{1,0:T(8,128)(2,1)} %param.40) | copy-start | bytes 6291460
  44.5 23.9 %copy-start.65 = (f32[512]{0:T(512)S(1)}, f32[512]{0:T(512)}, u32[]{:S(2)}) copy-start(f32[512]{0:T(512)} %param.41) | copy-start | bytes 6148
  71.1 78.3 %copy-start.55 = (s32[32]{0:T(128)S(1)}, s32[32]{0:T(128)}, u32[]{:S(2)}) copy-start(s32[32]{0:T(128)} %param.26) | copy-start | bytes 388
  71.2 78.2 %copy-start.59 = (s32[120]{0:T(128)S(1)}, s32[120]{0:T(128)}, u32[]{:S(2)}) copy-start(s32[120]{0:T(128)} %param.27) | copy-start | bytes 1444
  71.2 79.1 %copy-start.47 = (f32[32,120]{1,0:T(8,128)S(1)}, f32[32,120]{1,0:T(8,128)}, u32[]{:S(2)}) copy-start(f32[32,120]{1,0:T(8,128)} %param.28) | copy-start | bytes 46084
  152.1 652.8 %all-reduce.12.cloned.1.call-start = ((), (), s32[]{:S(2)}) async-start(), calls=%async_computation.1 | async-start | bytes 25165824 | tf_op jit(solution)/shard_map/psum | solution.py:257
  289.9 9.7 copy-start.13
  303.2 9.3 slice-start.4
  303.3 9.3 slice-start.5
  322.3 16.0 %copy-start.11 = (bf16[1024,512]{0,1:T(8,128)(2,1)S(1)}, bf16[1024,512]{0,1:T(8,128)(2,1)}, u32[]{:S(2)}) copy-start(bf16[1024,512]{0,1:T(8,128)(2,1)} %copy-done.10) | copy-start | bytes 3145732
  322.3 30.5 %slice-start = ((s8[16777216]{0:T(1024)(128)(4,1)}), s8[4194304]{0:T(1024)(128)(4,1)S(1)}, s32[]{:S(2)}) async-start(s8[16777216]{0:T(1024)(128)(4,1)} %bitcast.117), calls=%async_computation.3 | async-start | bytes 8388608
  322.3 30.5 %slice-start.1 = ((s8[16777216]{0:T(1024)(128)(4,1)}), s8[4194304]{0:T(1024)(128)(4,1)S(1)}, s32[]{:S(2)}) async-start(s8[16777216]{0:T(1024)(128)(4,1)} %bitcast.117), calls=%async_computation.4 | async-start | bytes 8388608
  322.4 30.5 %slice-start.2 = ((s8[16777216]{0:T(1024)(128)(4,1)}), s8[4194304]{0:T(1024)(128)(4,1)S(1)}, s32[]{:S(2)}) async-start(s8[16777216]{0:T(1024)(128)(4,1)} %bitcast.117), calls=%async_computation.5 | async-start | bytes 8388608
  338.3 8.2 copy-start.17
  338.3 14.5 %slice-start.3 = ((s8[16777216]{0:T(1024)(128)(4,1)}), s8[4194304]{0:T(1024)(128)(4,1)S(1)}, s32[]{:S(2)}) async-start(s8[16777216]{0:T(1024)(128)(4,1)} %bitcast.117), calls=%async_computation.6 | async-start | bytes 8388608
  346.5 6.4 copy-start.18
  346.5 6.4 copy-start.38
  366.8 8.8 copy-start.28
  366.8 10.5 %copy-start.40 = (f32[8,512]{1,0:T(8,128)S(1)}, f32[8,512]{1,0:T(8,128)}, u32[]{:S(2)}) copy-start(f32[8,512]{1,0:T(8,128)} %log_add_fusion) | copy-start | bytes 49156
  366.8 10.5 %copy-start.41 = (f32[8,512]{1,0:T(8,128)S(1)}, f32[8,512]{1,0:T(8,128)}, u32[]{:S(2)}) copy-start(f32[8,512]{1,0:T(8,128)} %get-tuple-element.151) | copy-start | bytes 49156
  387.8 6.3 copy-start.4
  387.8 6.3 copy-start.15
  400.9 629.0 %all-reduce.14.cloned.1.call-start = ((), (), s32[]{:S(2)}) async-start(), calls=%async_computation.2 | async-start | bytes 25165824 | tf_op jit(solution)/shard_map/psum | solution.py:256
  1029.9 6.5 copy-start.30
  1037.4 6.9 copy-start.1
  (48 other events, 169.7 us)
Sparse Core Ops, SparseCore 0:
  152.2 121.7 all-reduce.9
  401.1 403.7 all-reduce.11
  808.0 221.8 all-reduce.13
